TPU v7x, 32 devices: a whole 2x2x4 slice. The times are simulated.
32 devices in a mesh: layer: 4 (over x, core), feat: 8 (over z, y).
Axes of the slice: x: 2, y: 2, z: 4, core: 2. Of those that a mesh axis runs over, the one named last changes fastest.
Arguments:
- gradient: bfloat16 [4, 2560, 2560], P('layer', 'feat'), may hold values from -3 to 3
- in_inverse: bfloat16 [4, 2560, 2560], P('layer', 'feat'), may hold values from -1 to 2.5, as said below
- in_coupling: bfloat16 [4, 2560, 2560], P('layer', 'feat'), may hold values from -0.125 to 0.125
- in_carry: bfloat16 [4, 2560, 2560], P('layer', 'feat'), may hold values from -0.125 to 0.125
- out_inverse: bfloat16 [4, 20, 128, 128], P('layer'), may hold values from -1 to 2.5, as said below
- out_coupling: bfloat16 [4, 20, 128, 128], P('layer'), may hold values from -0.5 to 0.5
Outputs:
- update: bfloat16 [4, 2560, 2560], P('layer', 'feat')
Inputs may be any that keep to these rules, and one draw needn't show every extreme that they name: `in_inverse`: symmetric in its last two dimensions. `out_inverse`: symmetric in its last two dimensions.
All inputs are finite; a program needn't handle non-finite values.
Results may differ from a plain program's by a relative error of at most 0.006.
Values may be sent and summed in bfloat16 or wider, within the bound.
A program may use at most 64 MiB of HBM per device.

v0:
```python
import functools

import jax
import jax.numpy as jnp
from jax import lax
from jax.experimental import pallas as pl
from jax.experimental.pallas import tpu as pltpu
from jax.sharding import PartitionSpec as P

MESH = pl.DeviceIdType.MESH
BF = jnp.bfloat16
F32 = jnp.float32


def kernel(nl, nb, nch, lent, g_ref, s_ref, c_ref, k_ref, oi_ref, ps_ref, out_ref,
           w, gl, gn, tab, n_all, r_all, l_st, p_st, l_in, p_in, w2, gl2, gn2, l_st2, p_st2,
           w_recv, w_send, w_fwd, gl_recv, gl_send, gn_recv, gn_send, t_recv, t_send,
           n_recv, n_send, r_recv, r_send, l_recv, l_send, p_recv, p_send,
           w2_recv, w2_send, w2_fwd, gl2_recv, gl2_send, gn2_recv, gn2_send, l2_send, p2_send):
    r, d = out_ref.shape
    h = d // 2
    cw = h // nch
    blk = ps_ref.shape[1]
    hb = ps_ref.shape[0] // 2
    per = cw // blk
    l = lax.axis_index("layer")
    f = lax.axis_index("feat")
    a, c = l // 2, l % 2
    b, p = f // 2, f % 2
    role = 2 * a + p
    home = c == p
    away = c != p
    chained = role < nl - 1
    core_mate = (2 * a + 1 - c, f)
    swap_mate = (l, 2 * b + 1 - p)

    def remote(src, dst, ss, rs, dev):
        return pltpu.make_async_remote_copy(
            src_ref=src, dst_ref=dst, send_sem=ss, recv_sem=rs,
            device_id=dev, device_id_type=MESH)

    def arrived(dst, sem):
        pltpu.make_async_copy(dst, dst, sem).wait()

    barrier = pltpu.get_barrier_semaphore()
    for dl in range(1, nl):
        for q in range(2):
            pl.semaphore_signal(barrier, inc=1, device_id=(lax.rem(l + dl, nl), 2 * b + q), device_id_type=MESH)
    pl.semaphore_signal(barrier, inc=1, device_id=swap_mate, device_id_type=MESH)

    first_lent = nch - lent
    is_end = (b == 0) | (b == nb - 1)
    helps = (b == 1) | (b == nb - 2)
    mate_b = jnp.where((b == 0) | (b == nb - 1), jnp.where(b == 0, 1, nb - 2), jnp.where(b == 1, 0, nb - 1))
    if not lent:
        is_end = helps = b < 0
    paired = is_end | helps

    def mate(layer, q):
        return (layer, 2 * mate_b + q)

    @pl.when(paired)
    def _():
        for dl in range(nl):
            for q in range(2):
                pl.semaphore_signal(barrier, inc=1, device_id=mate(dl, q), device_id_type=MESH)

    low_plain = (b > 0) & jnp.logical_not(paired & (mate_b == b - 1))
    high_plain = (b < nb - 1) & jnp.logical_not(paired & (mate_b == b + 1))

    @pl.when(low_plain)
    def _():
        pl.semaphore_signal(barrier, inc=1, device_id=(l, f - 2), device_id_type=MESH)

    @pl.when(high_plain)
    def _():
        pl.semaphore_signal(barrier, inc=1, device_id=(l, f + 2), device_id_type=MESH)

    peers = 2 * nl - 1 + jnp.where(paired, 2 * nl, 0) + jnp.where(low_plain, 1, 0) + jnp.where(high_plain, 1, 0)
    pl.semaphore_wait(barrier, peers)

    low = l + nl - 1
    low_a, low_p = (low - nl) // 2, lax.rem(low, 2)

    def above_cols(hh, k):
        return g_ref.at[:, pl.ds(pl.multiple_of(hh * h + k * cw, cw), cw)]

    def above_stays(hh):
        return (l >= 1) & (c == 1) & (p == 0) & (c == hh)

    def above_copy(hh, k):
        return remote(above_cols(hh, k), gn.at[k, p], gn_send.at[k, hh], gn_recv.at[k, p],
                      (2 * low_a + hh, 2 * b + low_p))

    def send_above(k, carry):
        for hh in range(2):
            @pl.when(above_stays(hh))
            def _():
                pltpu.make_async_copy(above_cols(hh, k), gn.at[k, p], gn_recv.at[k, p]).start()

            @pl.when((l >= 1) & jnp.logical_not(above_stays(hh)))
            def _():
                above_copy(hh, k).start()
        return carry

    lax.fori_loop(0, nch, send_above, 0)

    @pl.when(home)
    def _():
        pltpu.make_async_copy(ps_ref.at[pl.ds(c * hb, hb)], tab.at[0], t_recv.at[0]).start()
        pltpu.make_async_copy(oi_ref.at[pl.ds(c * hb, hb)], tab.at[1], t_recv.at[1]).start()
        remote(ps_ref.at[pl.ds((1 - c) * hb, hb)], tab.at[0], t_send.at[0], t_recv.at[0], core_mate).start()
        remote(oi_ref.at[pl.ds((1 - c) * hb, hb)], tab.at[1], t_send.at[1], t_recv.at[1], core_mate).start()

    def g_half(hh):
        return g_ref.at[:, pl.ds(pl.multiple_of(hh * h, 128), h)]

    @pl.when(home)
    def _():
        pltpu.make_async_copy(g_half(c), gl.at[p], gl_recv.at[p]).start()
        remote(g_half(1 - c), gl.at[p], gl_send.at[0], gl_recv.at[p], core_mate).start()

    @pl.when(away)
    def _():
        remote(g_half(c), gl.at[p], gl_send.at[0], gl_recv.at[p], swap_mate).start()
        remote(g_half(1 - c), gl.at[p], gl_send.at[1], gl_recv.at[p], (2 * a + 1 - c, 2 * b + 1 - p)).start()

    weights = (c_ref, s_ref, k_ref)
    for m in range(3):
        @pl.when(home)
        def _():
            pltpu.make_async_copy(weights[m], w.at[m, p], w_recv.at[m, p]).start()
            remote(weights[m], w.at[m, p], w_send.at[m], w_recv.at[m, p], core_mate).start()

        @pl.when(away)
        def _():
            remote(weights[m], w.at[m, p], w_send.at[m], w_recv.at[m, p], swap_mate).start()

    def take_weight(m):
        arrived(w.at[m, 1 - p], w_recv.at[m, 1 - p])

        @pl.when(home)
        def _():
            remote(w.at[m, 1 - p], w.at[m, 1 - p], w_fwd.at[m], w_recv.at[m, 1 - p], core_mate).start()
        waited = home & is_end

        @pl.when(jnp.logical_not(waited))
        def _():
            arrived(w.at[m, p], w_recv.at[m, p])

    def hop(buf, k, src, up, send, recv):
        dev = (l, f + 2) if up else (l, f - 2)
        return remote(buf.at[k, src], buf.at[k, src], send.at[k, src, 0 if up else 1], recv.at[k, src], dev)

    def is_lent(k):
        return k >= first_lent

    def takes_part(k):
        return jnp.logical_not(is_lent(k) & is_end)

    def goes_up(k):
        return (b < nb - 1) & takes_part(k) & jnp.logical_not(is_lent(k) & (b + 1 == nb - 1))

    def goes_down(k):
        return (b > 0) & takes_part(k) & jnp.logical_not(is_lent(k) & (b - 1 == 0))

    def made_here(k, src):
        return is_lent(k) & helps & (src == mate_b)

    def pass_on(buf, send, recv, live, k, j):
        ok = live & (k >= 0) & (k < nch) & takes_part(k)
        if j == 0:
            @pl.when(ok & goes_up(k))
            def _():
                hop(buf, k, b, True, send, recv).start()

            @pl.when(ok & goes_down(k))
            def _():
                hop(buf, k, b, False, send, recv).start()
        else:
            for src, there, onward, up in ((b - j, b - j >= 0, goes_up(k), True),
                                           (b + j, b + j < nb, goes_down(k), False)):
                @pl.when(ok & there & jnp.logical_not(made_here(k, src)))
                def _():
                    arrived(buf.at[k, src], recv.at[k, src])

                @pl.when(ok & there & onward)
                def _():
                    hop(buf, k, src, up, send, recv).start()

    def sent(buf, send, recv, live, k):
        for src in range(nb):
            @pl.when(live & (src <= b) & goes_up(k))
            def _():
                hop(buf, k, src, True, send, recv).wait_send()

            @pl.when(live & (src >= b) & goes_down(k))
            def _():
                hop(buf, k, src, False, send, recv).wait_send()

    def columns(k):
        return pl.ds(pl.multiple_of(k * cw, cw), cw)

    for i in range(2):
        arrived(tab.at[i], t_recv.at[i])

    def near_of(x, k):
        parts = [lax.dot_general(x[:, i * blk:(i + 1) * blk], tab[0, k * per + i],
                                 (((1,), (1,)), ((), ())), preferred_element_type=F32).astype(BF)
                 for i in range(per)]
        return jnp.concatenate(parts, axis=1)

    def lend_above(k):
        return remote(gn.at[k], gn2.at[k - first_lent], gn2_send.at[k - first_lent],
                      gn2_recv.at[k - first_lent], mate(l, p))

    def lend_own():
        cols = pl.ds(first_lent * cw, lent * cw)
        return remote(gl.at[:, :, cols], gl2, gl2_send, gl2_recv, mate(l, p))

    def lend_weight(m, q):
        return remote(w.at[m, q], w2.at[m, q], w2_send.at[m, q], w2_recv.at[m, q], mate(l, p))

    def share_weight(m, q):
        return remote(w2.at[m, q], w2.at[m, q], w2_fwd.at[m, q], w2_recv.at[m, q], core_mate)

    def take_lent(m):
        for q in range(2):
            arrived(w2.at[m, q], w2_recv.at[m, q])

            @pl.when(home)
            def _():
                share_weight(m, q).start()

    def near_step(k):
        for q in range(2):
            arrived(gn.at[k, q], gn_recv.at[k, q])

        @pl.when(takes_part(k))
        def _():
            n_all[k, b] = near_of(gn[k].reshape(2 * r, cw), k)

        if lent:
            @pl.when(jnp.logical_not(takes_part(k)))
            def _():
                lend_above(k).start()

    def near_lent(k):
        i = k - first_lent
        arrived(gn2.at[i], gn2_recv.at[i])
        n_all[k, mate_b] = near_of(gn2[i].reshape(2 * r, cw), k)

    def reduced_lent(k):
        cols = pl.ds(pl.multiple_of((k - first_lent) * cw, cw), cw)

        @pl.when(k == first_lent)
        def _():
            arrived(gl2, gl2_recv)

        @pl.when(chained)
        def _():
            x = n_all[k].reshape(nb * 2 * r, cw)
            coupled = jnp.dot(w2[0].reshape(2 * r, d), x, preferred_element_type=F32)
            r_all[k, mate_b] = (gl2[:, :, cols].reshape(2 * r, cw).astype(F32) - coupled).astype(BF)

        @pl.when(jnp.logical_not(chained))
        def _():
            r_all[k, mate_b] = gl2[:, :, cols].reshape(2 * r, cw)

    def local_lent(k, q):
        i = k - first_lent
        return remote(l_st2.at[i, q], l_in.at[k, c], l2_send.at[i, q], l_recv.at[k, c], mate(role, q))

    def push_lent(k, q):
        i = k - first_lent
        return remote(p_st2.at[i, q], p_in.at[k, c], p2_send.at[i, q], p_recv.at[k, c],
                      mate(lax.rem(role + 1, nl), q))

    def final_lent(k):
        i = k - first_lent
        x = r_all[k].reshape(nb * 2 * r, cw)
        white = jnp.dot(w2[1].reshape(2 * r, d), x, preferred_element_type=F32).astype(BF)
        for n in range(per):
            o = jnp.dot(white[:, n * blk:(n + 1) * blk], tab[1, k * per + n], preferred_element_type=F32)
            l_st2[i, :, :, n * blk:(n + 1) * blk] = o.astype(BF).reshape(2, r, blk)
        for q in range(2):
            local_lent(k, q).start()

        @pl.when(chained)
        def _():
            y = r_all[k].reshape(nb * 2 * r, cw)
            carried = jnp.dot(w2[2].reshape(2 * r, d), y, preferred_element_type=F32).astype(BF)
            for n in range(per):
                mid = jnp.dot(carried[:, n * blk:(n + 1) * blk], tab[1, k * per + n],
                              preferred_element_type=F32).astype(BF)
                o = jnp.dot(mid, tab[0, k * per + n], preferred_element_type=F32)
                p_st2[i, :, :, n * blk:(n + 1) * blk] = o.astype(BF).reshape(2, r, blk)
            for q in range(2):
                push_lent(k, q).start()

    def reduced_step(k):
        @pl.when(chained)
        def _():
            x = n_all[k].reshape(nb * 2 * r, cw)
            coupled = jnp.dot(w[0].reshape(2 * r, d), x, preferred_element_type=F32)
            g = gl[:, :, columns(k)].reshape(2 * r, cw).astype(F32)
            r_all[k, b] = (g - coupled).astype(BF)

        @pl.when(jnp.logical_not(chained))
        def _():
            r_all[k, b] = gl[:, :, columns(k)].reshape(2 * r, cw)

    def local_copy(k, q):
        return remote(l_st.at[k, q], l_in.at[k, c], l_send.at[k, q], l_recv.at[k, c], (role, 2 * b + q))

    def push_copy(k, q):
        return remote(p_st.at[k, q], p_in.at[k, c], p_send.at[k, q], p_recv.at[k, c],
                      (lax.rem(role + 1, nl), 2 * b + q))

    def stays(q, layer):
        return (l == layer) & (p == q)

    def final_step(k):
        x = r_all[k].reshape(nb * 2 * r, cw)
        white = jnp.dot(w[1].reshape(2 * r, d), x, preferred_element_type=F32).astype(BF)
        for i in range(per):
            o = jnp.dot(white[:, i * blk:(i + 1) * blk], tab[1, k * per + i], preferred_element_type=F32)
            l_st[k, :, :, i * blk:(i + 1) * blk] = o.astype(BF).reshape(2, r, blk)
        for q in range(2):
            @pl.when(stays(q, role))
            def _():
                pltpu.make_async_copy(l_st.at[k, q], l_in.at[k, c], l_recv.at[k, c]).start()

            @pl.when(jnp.logical_not(stays(q, role)))
            def _():
                local_copy(k, q).start()

        @pl.when(chained)
        def _():
            y = r_all[k].reshape(nb * 2 * r, cw)
            carried = jnp.dot(w[2].reshape(2 * r, d), y, preferred_element_type=F32).astype(BF)
            for i in range(per):
                mid = jnp.dot(carried[:, i * blk:(i + 1) * blk], tab[1, k * per + i],
                              preferred_element_type=F32).astype(BF)
                o = jnp.dot(mid, tab[0, k * per + i], preferred_element_type=F32)
                p_st[k, :, :, i * blk:(i + 1) * blk] = o.astype(BF).reshape(2, r, blk)
            for q in range(2):
                @pl.when(stays(q, role + 1))
                def _():
                    pltpu.make_async_copy(p_st.at[k, q], p_in.at[k, c], p_recv.at[k, c]).start()

                @pl.when(jnp.logical_not(stays(q, role + 1)))
                def _():
                    push_copy(k, q).start()

    def out_step(k):
        for hh in range(2):
            arrived(l_in.at[k, hh], l_recv.at[k, hh])
            dst = pl.ds(pl.multiple_of(hh * h + k * cw, cw), cw)

            @pl.when(l > 0)
            def _():
                arrived(p_in.at[k, hh], p_recv.at[k, hh])
                out_ref[:, dst] = (l_in[k, hh].astype(F32) - p_in[k, hh].astype(F32)).astype(BF)

            @pl.when(l == 0)
            def _():
                out_ref[:, dst] = l_in[k, hh]

    def inside(k):
        return (k >= 0) & (k < nch)

    n_lag = nb - 1
    r_lag = 2 * (nb - 1)

    def step(t, carry):
        @pl.when(chained & inside(t))
        def _():
            near_step(t)
        if lent:
            @pl.when(chained & helps & inside(t - 1) & is_lent(t - 1))
            def _():
                near_lent(t - 1)
        for j in range(nb):
            pass_on(n_all, n_send, n_recv, chained, t - j, j)
        kr = t - n_lag

        @pl.when(kr == 0)
        def _():
            for q in range(2):
                arrived(gl.at[q], gl_recv.at[q])
            take_weight(0)
        if lent:
            @pl.when((kr == 0) & is_end)
            def _():
                lend_own().start()

            @pl.when((kr == first_lent) & helps)
            def _():
                take_lent(0)

        @pl.when(inside(kr) & takes_part(kr))
        def _():
            reduced_step(kr)
        if lent:
            @pl.when(helps & inside(kr - 1) & is_lent(kr - 1))
            def _():
                reduced_lent(kr - 1)
        for j in range(nb):
            pass_on(r_all, r_send, r_recv, True, kr - j, j)

        if lent:
            for m in range(3):
                @pl.when((t == m + 2) & home & is_end)
                def _():
                    arrived(w.at[m, p], w_recv.at[m, p])
                    lend_weight(m, p).start()

                if m == 0:
                    @pl.when((kr == 0) & home & is_end)
                    def _():
                        lend_weight(m, 1 - p).start()
        kf = t - r_lag

        @pl.when(kf == 0)
        def _():
            take_weight(1)
            take_weight(2)
        if lent:
            for m in range(1, 3):
                @pl.when((kf == 0) & home & is_end)
                def _():
                    lend_weight(m, 1 - p).start()

                @pl.when((kf == first_lent) & helps)
                def _():
                    take_lent(m)

        if lent:
            @pl.when(helps & inside(kf) & is_lent(kf))
            def _():
                final_lent(kf)

        @pl.when(inside(kf) & takes_part(kf))
        def _():
            final_step(kf)
        ko = kf - 1

        @pl.when(inside(ko))
        def _():
            out_step(ko)
        return carry

    lax.fori_loop(0, nch + r_lag + 1, step, 0)

    def drain(k, carry):
        sent(n_all, n_send, n_recv, chained, k)
        sent(r_all, r_send, r_recv, True, k)
        for q in range(2):
            @pl.when((l >= 1) & jnp.logical_not(above_stays(q)))
            def _():
                above_copy(q, k).wait_send()

            @pl.when(takes_part(k) & jnp.logical_not(stays(q, role)))
            def _():
                local_copy(k, q).wait_send()

            @pl.when(takes_part(k) & chained & jnp.logical_not(stays(q, role + 1)))
            def _():
                push_copy(k, q).wait_send()

            if lent:
                @pl.when(is_lent(k) & helps)
                def _():
                    local_lent(k, q).wait_send()

                @pl.when(is_lent(k) & helps & chained)
                def _():
                    push_lent(k, q).wait_send()
        if lent:
            @pl.when(chained & jnp.logical_not(takes_part(k)))
            def _():
                lend_above(k).wait_send()
        return carry

    lax.fori_loop(0, nch, drain, 0)
    if lent:
        @pl.when(is_end)
        def _():
            lend_own().wait_send()
        for m in range(3):
            for q in range(2):
                @pl.when(home & is_end)
                def _():
                    lend_weight(m, q).wait_send()

                @pl.when(home & helps)
                def _():
                    share_weight(m, q).wait_send()

    @pl.when(home)
    def _():
        for i, src in enumerate((ps_ref, oi_ref)):
            remote(src.at[pl.ds((1 - c) * hb, hb)], tab.at[i], t_send.at[i], t_recv.at[i], core_mate).wait_send()
        remote(g_half(1 - c), gl.at[p], gl_send.at[0], gl_recv.at[p], core_mate).wait_send()
        for m in range(3):
            remote(w.at[m, 1 - p], w.at[m, 1 - p], w_fwd.at[m], w_recv.at[m, 1 - p], core_mate).wait_send()

    @pl.when(away)
    def _():
        remote(g_half(c), gl.at[p], gl_send.at[0], gl_recv.at[p], swap_mate).wait_send()
        remote(g_half(1 - c), gl.at[p], gl_send.at[1], gl_recv.at[p], swap_mate).wait_send()
    for m in range(3):
        remote(weights[m], w.at[m, p], w_send.at[m], w_recv.at[m, p], core_mate).wait_send()


def local(nl, nf, gradient, in_inverse, in_coupling, in_carry, out_inverse, out_coupling):
    g = gradient[0]
    r, d = g.shape
    nb = nf // 2
    blocks, blk = out_inverse.shape[1], out_inverse.shape[2]
    h = d // 2
    hb = blocks // 2
    nch = hb // 2 if hb % 2 == 0 else hb
    cw = h // nch
    lent = 1 if nb >= 4 and nch >= 5 else 0
    keep = max(lent, 1)
    dma = pltpu.SemaphoreType.DMA
    vm = pltpu.VMEM
    anyspec = pl.BlockSpec(memory_space=pl.ANY)
    out = pl.pallas_call(
        functools.partial(kernel, nl, nb, nch, lent),
        out_shape=jax.ShapeDtypeStruct((r, d), BF),
        in_specs=[anyspec] * 6,
        out_specs=pl.BlockSpec(memory_space=pltpu.VMEM),
        scratch_shapes=[
            vm((3, 2, r, d), BF), vm((2, r, h), BF), vm((nch, 2, r, cw), BF), vm((2, hb, blk, blk), BF),
            vm((nch, nb, 2 * r, cw), BF), vm((nch, nb, 2 * r, cw), BF),
            vm((nch, 2, r, cw), BF), vm((nch, 2, r, cw), BF), vm((nch, 2, r, cw), BF), vm((nch, 2, r, cw), BF),
            vm((3, 2, r, d), BF), vm((2, r, keep * cw), BF), vm((keep, 2, r, cw), BF),
            vm((keep, 2, r, cw), BF), vm((keep, 2, r, cw), BF),
            dma((3, 2)), dma((3,)), dma((3,)), dma((2,)), dma((2,)), dma((nch, 2)), dma((nch, 2)), dma((2,)), dma((2,)),
            dma((nch, nb)), dma((nch, nb, 2)), dma((nch, nb)), dma((nch, nb, 2)),
            dma((nch, 2)), dma((nch, 2)), dma((nch, 2)), dma((nch, 2)),
            dma((3, 2)), dma((3, 2)), dma((3, 2)), dma, dma, dma((keep,)), dma((keep,)), dma((keep, 2)), dma((keep, 2)),
        ],
        compiler_params=pltpu.CompilerParams(
            collective_id=0, has_side_effects=True, vmem_limit_bytes=62 * 1024 * 1024),
    )(g, in_inverse[0], in_coupling[0], in_carry[0], out_inverse[0], out_coupling[0])
    return out[None]


def solution(mesh):
    return jax.shard_map(
        functools.partial(local, mesh.shape["layer"], mesh.shape["feat"]),
        mesh=mesh,
        in_specs=(
            P("layer", "feat", None),
            P("layer", "feat", None),
            P("layer", "feat", None),
            P("layer", "feat", None),
            P("layer", None, None, None),
            P("layer", None, None, None),
        ),
        out_specs=P("layer", "feat", None),
        check_vma=False,
    )
```

profile of v0, /device:TPU:7, one launch (start us, length us, event | category | flops | bytes accessed | tf_op | source)
XLA Modules:
  0.0 213.7 jit_solution(16246616307350558431)
XLA Ops:
  0.0 211.0 %shard_map.64 = bf16[320,2560]{1,0:T(8,128)(2,1)} custom-call(bf16[320,2560]{1,0:T(8,128)(2,1)} %bitcast.8, bf16[320,2560]{1,0:T(8,128)(2,1)} %bitcast.9, bf16[320,2560]{1,0:T(8,128)(2,1)} %bitcast.10, bf16[320,2560]{1,0:T(8,128)(2,1)} %bitcast.11, bf16[20,128,128]{2,1,0:T(8,128)(2,1)} %bitcast.12, bf16[20,128,128]{2,1,0:T(8,128)(2,1)} %bitcast.13), custom_call_target="tpu_custom_call" | custom-call | tf_op jit(solution)/shard_map/pallas_call | solution.py:531
  211.0 2.7 %copy.8 = bf16[1,320,2560]{2,1,0:T(8,128)(2,1)} copy(bf16[1,320,2560]{2,1,0:T(8,128)(2,1)} %bitcast.7) | data formatting | bytes 3276800
where the time goes:
time: 215 us; the launch traced here: 214 us
  Pallas kernels  211 us (98%)
  local copies, waits for them, and re-layouts  2.7 us (1%)
    pallas_call x1, Pallas kernels, local(): pl.pallas_call(functools.partial(kernel, nl, nb, nch, lent), out_shape=ja...  211 us

commit v1 on v0

v1 whole, which is shorter than its diff:
```python
import functools

import jax
import jax.numpy as jnp
from jax import lax
from jax.experimental import pallas as pl
from jax.experimental.pallas import tpu as pltpu
from jax.sharding import PartitionSpec as P

MESH = pl.DeviceIdType.MESH
BF = jnp.bfloat16
F32 = jnp.float32
LENT = 7
HOLD = 3


def kernel(nl, nb, nch, lent, g_ref, s_ref, c_ref, k_ref, oi_ref, ps_ref, out_ref,
           w, gl, gn, tab, n_all, r_all, l_st, p_st, l_in, p_in, w2, gl2,
           w_recv, w_send, w_fwd, gl_recv, gl_send, gn_recv, gn_send, t_recv, t_send,
           n_recv, n_send, r_recv, r_send, l_recv, l_send, p_recv, p_send,
           w2_recv, w2_send, w2_fwd, w2_got, gl2_recv, gl2_send):
    r, d = out_ref.shape
    h = d // 2
    cw = h // nch
    blk = ps_ref.shape[1]
    hb = ps_ref.shape[0] // 2
    per = cw // blk
    l = lax.axis_index("layer")
    f = lax.axis_index("feat")
    a, c = l // 2, l % 2
    b, p = f // 2, f % 2
    role = 2 * a + p
    home = c == p
    away = c != p
    chained = role < nl - 1
    core_mate = (2 * a + 1 - c, f)
    swap_mate = (l, 2 * b + 1 - p)
    n_lag = nb - 1
    r_lag = 2 * (nb - 1)
    ahead = min(4, nch)
    first_lent = nch - lent
    halves = w2_send.shape[0]
    piece = r // halves

    def remote(src, dst, ss, rs, dev):
        return pltpu.make_async_remote_copy(
            src_ref=src, dst_ref=dst, send_sem=ss, recv_sem=rs,
            device_id=dev, device_id_type=MESH)

    def arrived(dst, sem):
        pltpu.make_async_copy(dst, dst, sem).wait()

    barrier = pltpu.get_barrier_semaphore()
    for dl in range(1, nl):
        for q in range(2):
            pl.semaphore_signal(barrier, inc=1, device_id=(lax.rem(l + dl, nl), 2 * b + q), device_id_type=MESH)
    pl.semaphore_signal(barrier, inc=1, device_id=swap_mate, device_id_type=MESH)

    @pl.when(b > 0)
    def _():
        pl.semaphore_signal(barrier, inc=1, device_id=(l, f - 2), device_id_type=MESH)

    @pl.when(b < nb - 1)
    def _():
        pl.semaphore_signal(barrier, inc=1, device_id=(l, f + 2), device_id_type=MESH)

    pl.semaphore_wait(barrier, 2 * nl - 1 + jnp.where(b > 0, 1, 0) + jnp.where(b < nb - 1, 1, 0))

    is_end = (b == 0) | (b == nb - 1)
    helps = (b == 1) | (b == nb - 2)
    if not lent:
        is_end = helps = b < 0
    mate_b = jnp.where(b < 2, 1 - b, 2 * nb - 3 - b)
    mate = (l, 2 * mate_b + p)

    def is_lent(k):
        return chained & (k >= first_lent)

    low = l + nl - 1
    low_a, low_p = (low - nl) // 2, lax.rem(low, 2)

    def own_cols(hh, k):
        return g_ref.at[:, pl.ds(pl.multiple_of(hh * h + k * cw, cw), cw)]

    def above_stays(hh):
        return (l >= 1) & (c == 1) & (p == 0) & (c == hh)

    def above_copy(hh, k):
        return remote(own_cols(hh, k), gn.at[k, p], gn_send.at[k, hh], gn_recv.at[k, p],
                      (2 * low_a + hh, 2 * b + low_p))

    def send_above(k, carry):
        for hh in range(2):
            @pl.when(above_stays(hh))
            def _():
                pltpu.make_async_copy(own_cols(hh, k), gn.at[k, p], gn_recv.at[k, p]).start()

            @pl.when((l >= 1) & jnp.logical_not(above_stays(hh)))
            def _():
                above_copy(hh, k).start()
        return carry

    def own_to(hh, k, i, dev):
        return remote(own_cols(hh, k), gl.at[k, p], gl_send.at[k, i], gl_recv.at[k, p], dev)

    def send_own(k, carry):
        @pl.when(home)
        def _():
            pltpu.make_async_copy(own_cols(c, k), gl.at[k, p], gl_recv.at[k, p]).start()
            own_to(1 - c, k, 0, core_mate).start()

        @pl.when(away)
        def _():
            own_to(c, k, 0, swap_mate).start()
            own_to(1 - c, k, 1, (2 * a + 1 - c, 2 * b + 1 - p)).start()
        return carry

    weights = (c_ref, s_ref, k_ref)

    def used(m, layer):
        return (layer < nl - 1) | (m == 1)

    def send_weight(m):
        @pl.when(home & used(m, l))
        def _():
            pltpu.make_async_copy(weights[m], w.at[m, p], w_recv.at[m, p]).start()
            remote(weights[m], w.at[m, p], w_send.at[m], w_recv.at[m, p], core_mate).start()

        @pl.when(away & used(m, l))
        def _():
            remote(weights[m], w.at[m, p], w_send.at[m], w_recv.at[m, p], swap_mate).start()

    lax.fori_loop(0, ahead, send_above, 0)

    @pl.when(home)
    def _():
        pltpu.make_async_copy(ps_ref.at[pl.ds(c * hb, hb)], tab.at[0], t_recv.at[0]).start()
        pltpu.make_async_copy(oi_ref.at[pl.ds(c * hb, hb)], tab.at[1], t_recv.at[1]).start()
        remote(ps_ref.at[pl.ds((1 - c) * hb, hb)], tab.at[0], t_send.at[0], t_recv.at[0], core_mate).start()
        remote(oi_ref.at[pl.ds((1 - c) * hb, hb)], tab.at[1], t_send.at[1], t_recv.at[1], core_mate).start()

    lax.fori_loop(0, ahead, send_own, 0)
    send_weight(0)
    lax.fori_loop(ahead, nch, send_own, 0)
    send_weight(1)
    send_weight(2)

    def take_weight(m, early):
        @pl.when(used(m, role))
        def _():
            arrived(w.at[m, 1 - p], w_recv.at[m, 1 - p])

            @pl.when(home)
            def _():
                remote(w.at[m, 1 - p], w.at[m, 1 - p], w_fwd.at[m], w_recv.at[m, 1 - p], core_mate).start()

            @pl.when((not early) | away)
            def _():
                arrived(w.at[m, p], w_recv.at[m, p])

    def hop(buf, k, src, up, send, recv):
        dev = (l, f + 2) if up else (l, f - 2)
        return remote(buf.at[k, src], buf.at[k, src], send.at[k, src, 0 if up else 1], recv.at[k, src], dev)

    def n_up(k):
        return (b < nb - 1) & jnp.logical_not(is_lent(k) & (b + 1 == nb - 1))

    def n_down(k):
        return (b > 0) & jnp.logical_not(is_lent(k) & (b - 1 == 0))

    def inside(k):
        return (k >= 0) & (k < nch)

    def pass_near(k, j):
        ok = chained & inside(k)
        if j == 0:
            @pl.when(ok & n_up(k))
            def _():
                hop(n_all, k, b, True, n_send, n_recv).start()

            @pl.when(ok & n_down(k))
            def _():
                hop(n_all, k, b, False, n_send, n_recv).start()
        else:
            takes = ok & jnp.logical_not(is_lent(k) & is_end)
            for src, there, onward, up in ((b - j, b - j >= 0, n_up(k), True),
                                           (b + j, b + j < nb, n_down(k), False)):
                @pl.when(takes & there)
                def _():
                    arrived(n_all.at[k, src], n_recv.at[k, src])

                @pl.when(takes & there & onward)
                def _():
                    hop(n_all, k, src, up, n_send, n_recv).start()

    def pass_reduced(k, j):
        ok = inside(k)
        if j == 0:
            makes = ok & jnp.logical_not(is_lent(k) & is_end)

            @pl.when(makes & (b < nb - 1))
            def _():
                hop(r_all, k, b, True, r_send, r_recv).start()

            @pl.when(makes & (b > 0))
            def _():
                hop(r_all, k, b, False, r_send, r_recv).start()
        else:
            if j == 1:
                @pl.when(ok & is_lent(k) & is_end)
                def _():
                    arrived(r_all.at[k, b], r_recv.at[k, b])
            for src, there, onward, up in ((b - j, b - j >= 0, b < nb - 1, True),
                                           (b + j, b + j < nb, b > 0, False)):
                comes = ok & there & jnp.logical_not(is_lent(k) & helps & (src == mate_b))

                @pl.when(comes)
                def _():
                    arrived(r_all.at[k, src], r_recv.at[k, src])

                @pl.when(comes & onward)
                def _():
                    hop(r_all, k, src, up, r_send, r_recv).start()

    for i in range(2):
        arrived(tab.at[i], t_recv.at[i])

    def near_step(k):
        for q in range(2):
            arrived(gn.at[k, q], gn_recv.at[k, q])
        x = gn[k].reshape(2 * r, cw)
        parts = [lax.dot_general(x[:, i * blk:(i + 1) * blk], tab[0, k * per + i],
                                 (((1,), (1,)), ((), ())), preferred_element_type=F32).astype(BF)
                 for i in range(per)]
        n_all[k, b] = jnp.concatenate(parts, axis=1) if per > 1 else parts[0]

    def lend_own(k):
        return remote(gl.at[k], gl2.at[k - first_lent], gl2_send.at[k - first_lent],
                      gl2_recv.at[k - first_lent], mate)

    def rows(i):
        return pl.ds(i * piece, piece)

    def lend_weight(i):
        return remote(w.at[0, c, rows(i)], w2.at[c, rows(i)], w2_send.at[i], w2_recv.at[i], mate)

    def share_weight(i):
        return remote(w2.at[c, rows(i)], w2.at[c, rows(i)], w2_fwd.at[i], w2_got.at[i], core_mate)

    def take_own(k):
        for q in range(2):
            arrived(gl.at[k, q], gl_recv.at[k, q])

    def reduced_step(k):
        @pl.when(chained)
        def _():
            x = n_all[k].reshape(nb * 2 * r, cw)
            coupled = jnp.dot(w[0].reshape(2 * r, d), x, preferred_element_type=F32)
            r_all[k, b] = (gl[k].reshape(2 * r, cw).astype(F32) - coupled).astype(BF)

        @pl.when(jnp.logical_not(chained))
        def _():
            r_all[k, b] = gl[k].reshape(2 * r, cw)

    def reduced_lent(k):
        i = k - first_lent
        arrived(gl2.at[i], gl2_recv.at[i])
        x = n_all[k].reshape(nb * 2 * r, cw)
        coupled = jnp.dot(w2[...].reshape(2 * r, d), x, preferred_element_type=F32)
        r_all[k, mate_b] = (gl2[i].reshape(2 * r, cw).astype(F32) - coupled).astype(BF)
        for up in (True, False):
            hop(r_all, k, mate_b, up, r_send, r_recv).start()

    def local_copy(k, q):
        return remote(l_st.at[k, q], l_in.at[k, c], l_send.at[k, q], l_recv.at[k, c], (role, 2 * b + q))

    def push_copy(k, q):
        return remote(p_st.at[k, q], p_in.at[k, c], p_send.at[k, q], p_recv.at[k, c],
                      (lax.rem(role + 1, nl), 2 * b + q))

    def stays(q, layer):
        return (l == layer) & (p == q)

    def final_step(k, carry):
        x = r_all[k].reshape(nb * 2 * r, cw)
        white = jnp.dot(w[1].reshape(2 * r, d), x, preferred_element_type=F32).astype(BF)
        for i in range(per):
            o = jnp.dot(white[:, i * blk:(i + 1) * blk], tab[1, k * per + i], preferred_element_type=F32)
            l_st[k, :, :, i * blk:(i + 1) * blk] = o.astype(BF).reshape(2, r, blk)
        for q in range(2):
            @pl.when(stays(q, role))
            def _():
                pltpu.make_async_copy(l_st.at[k, q], l_in.at[k, c], l_recv.at[k, c]).start()

            @pl.when(jnp.logical_not(stays(q, role)))
            def _():
                local_copy(k, q).start()

        @pl.when(chained)
        def _():
            y = r_all[k].reshape(nb * 2 * r, cw)
            carried = jnp.dot(w[2].reshape(2 * r, d), y, preferred_element_type=F32).astype(BF)
            for i in range(per):
                mid = jnp.dot(carried[:, i * blk:(i + 1) * blk], tab[1, k * per + i],
                              preferred_element_type=F32).astype(BF)
                o = jnp.dot(mid, tab[0, k * per + i], preferred_element_type=F32)
                p_st[k, :, :, i * blk:(i + 1) * blk] = o.astype(BF).reshape(2, r, blk)
            for q in range(2):
                @pl.when(stays(q, role + 1))
                def _():
                    pltpu.make_async_copy(p_st.at[k, q], p_in.at[k, c], p_recv.at[k, c]).start()

                @pl.when(jnp.logical_not(stays(q, role + 1)))
                def _():
                    push_copy(k, q).start()
        return carry

    def out_step(k, carry):
        for hh in range(2):
            arrived(l_in.at[k, hh], l_recv.at[k, hh])
            dst = pl.ds(pl.multiple_of(hh * h + k * cw, cw), cw)

            @pl.when(l > 0)
            def _():
                arrived(p_in.at[k, hh], p_recv.at[k, hh])
                out_ref[:, dst] = (l_in[k, hh].astype(F32) - p_in[k, hh].astype(F32)).astype(BF)

            @pl.when(l == 0)
            def _():
                out_ref[:, dst] = l_in[k, hh]
        return carry

    held = r_lag + min(HOLD, nch // 2)

    def finals(t):
        return jnp.clip(jnp.minimum(t - r_lag + 1, 2 * (t - held + 1)), 0, nch)

    def step(t, carry):
        @pl.when(t + ahead < nch)
        def _():
            send_above(t + ahead, 0)

        @pl.when(chained & inside(t))
        def _():
            near_step(t)
        for j in range(nb):
            pass_near(t - j, j)

        @pl.when((t == 1) & home & used(0, role))
        def _():
            arrived(w.at[0, p], w_recv.at[0, p])
        kr = t - n_lag

        @pl.when(kr == 0)
        def _():
            take_weight(0, True)
        if lent:
            for i in range(halves):
                @pl.when(chained & is_end & (t == jnp.where(home, 1, n_lag) + i))
                def _():
                    lend_weight(i).start()

            @pl.when(is_end & inside(t - 1) & is_lent(t - 1))
            def _():
                take_own(t - 1)
                lend_own(t - 1).start()

            @pl.when(chained & helps & (kr == first_lent))
            def _():
                for i in range(halves):
                    arrived(w2.at[c, rows(i)], w2_recv.at[i])
                    share_weight(i).start()

        @pl.when(inside(kr) & jnp.logical_not(is_lent(kr) & is_end))
        def _():
            take_own(kr)
            reduced_step(kr)
        pass_reduced(kr, 0)
        if lent:
            @pl.when(chained & helps & (kr == first_lent))
            def _():
                for i in range(halves):
                    arrived(w2.at[1 - c, rows(i)], w2_got.at[i])

            @pl.when(helps & inside(kr) & is_lent(kr))
            def _():
                reduced_lent(kr)
        for j in range(1, nb):
            pass_reduced(kr - j, j)

        @pl.when(t == held)
        def _():
            take_weight(1, False)
            take_weight(2, False)
        lax.fori_loop(finals(t - 1), finals(t), final_step, 0)
        lax.fori_loop(finals(t - 2), finals(t - 1), out_step, 0)
        return carry

    lax.fori_loop(0, nch + r_lag + 1, step, 0)

    def drain(k, carry):
        for src in range(nb):
            @pl.when(chained & (src <= b) & n_up(k) & jnp.logical_not(is_lent(k) & is_end & (src != b)))
            def _():
                hop(n_all, k, src, True, n_send, n_recv).wait_send()

            @pl.when(chained & (src >= b) & n_down(k) & jnp.logical_not(is_lent(k) & is_end & (src != b)))
            def _():
                hop(n_all, k, src, False, n_send, n_recv).wait_send()
            kept = is_lent(k) & is_end & (src == b)
            made = is_lent(k) & helps & (src == mate_b)

            @pl.when((b < nb - 1) & (src <= b) & jnp.logical_not(kept) | made)
            def _():
                hop(r_all, k, src, True, r_send, r_recv).wait_send()

            @pl.when((b > 0) & (src >= b) & jnp.logical_not(kept) | made)
            def _():
                hop(r_all, k, src, False, r_send, r_recv).wait_send()
        for q in range(2):
            @pl.when((l >= 1) & jnp.logical_not(above_stays(q)))
            def _():
                above_copy(q, k).wait_send()

            @pl.when(jnp.logical_not(stays(q, role)))
            def _():
                local_copy(k, q).wait_send()

            @pl.when(chained & jnp.logical_not(stays(q, role + 1)))
            def _():
                push_copy(k, q).wait_send()
        own_to(c, k, 0, swap_mate).wait_send()

        @pl.when(away)
        def _():
            own_to(c, k, 1, swap_mate).wait_send()
        if lent:
            @pl.when(is_lent(k) & is_end)
            def _():
                lend_own(k).wait_send()
        return carry

    lax.fori_loop(0, nch, drain, 0)
    if lent:
        for i in range(halves):
            @pl.when(chained & is_end)
            def _():
                lend_weight(i).wait_send()

            @pl.when(chained & helps)
            def _():
                share_weight(i).wait_send()

    @pl.when(home)
    def _():
        for i, src in enumerate((ps_ref, oi_ref)):
            remote(src.at[pl.ds((1 - c) * hb, hb)], tab.at[i], t_send.at[i], t_recv.at[i], core_mate).wait_send()
    for m in range(3):
        @pl.when(home & used(m, role))
        def _():
            remote(w.at[m, 1 - p], w.at[m, 1 - p], w_fwd.at[m], w_recv.at[m, 1 - p], core_mate).wait_send()

        @pl.when(used(m, l))
        def _():
            remote(weights[m], w.at[m, p], w_send.at[m], w_recv.at[m, p], core_mate).wait_send()


def local(nl, nf, gradient, in_inverse, in_coupling, in_carry, out_inverse, out_coupling):
    g = gradient[0]
    r, d = g.shape
    nb = nf // 2
    blocks, blk = out_inverse.shape[1], out_inverse.shape[2]
    h = d // 2
    hb = blocks // 2
    nch = hb
    cw = h // nch
    lent = nch * LENT // 10 if nb >= 4 and nch >= 4 else 0
    keep = max(lent, 1)
    halves = 2 if r % 32 == 0 else 1
    dma = pltpu.SemaphoreType.DMA
    vm = pltpu.VMEM
    anyspec = pl.BlockSpec(memory_space=pl.ANY)
    out = pl.pallas_call(
        functools.partial(kernel, nl, nb, nch, lent),
        out_shape=jax.ShapeDtypeStruct((r, d), BF),
        in_specs=[anyspec] * 6,
        out_specs=pl.BlockSpec(memory_space=pltpu.VMEM),
        scratch_shapes=[
            vm((3, 2, r, d), BF), vm((nch, 2, r, cw), BF), vm((nch, 2, r, cw), BF), vm((2, hb, blk, blk), BF),
            vm((nch, nb, 2 * r, cw), BF), vm((nch, nb, 2 * r, cw), BF),
            vm((nch, 2, r, cw), BF), vm((nch, 2, r, cw), BF), vm((nch, 2, r, cw), BF), vm((nch, 2, r, cw), BF),
            vm((2, r, d), BF), vm((keep, 2, r, cw), BF),
            dma((3, 2)), dma((3,)), dma((3,)), dma((nch, 2)), dma((nch, 2)), dma((nch, 2)), dma((nch, 2)),
            dma((2,)), dma((2,)),
            dma((nch, nb)), dma((nch, nb, 2)), dma((nch, nb)), dma((nch, nb, 2)),
            dma((nch, 2)), dma((nch, 2)), dma((nch, 2)), dma((nch, 2)),
            dma((halves,)), dma((halves,)), dma((halves,)), dma((halves,)), dma((keep,)), dma((keep,)),
        ],
        compiler_params=pltpu.CompilerParams(
            collective_id=0, has_side_effects=True, vmem_limit_bytes=62 * 1024 * 1024),
    )(g, in_inverse[0], in_coupling[0], in_carry[0], out_inverse[0], out_coupling[0])
    return out[None]


def solution(mesh):
    return jax.shard_map(
        functools.partial(local, mesh.shape["layer"], mesh.shape["feat"]),
        mesh=mesh,
        in_specs=(
            P("layer", "feat", None),
            P("layer", "feat", None),
            P("layer", "feat", None),
            P("layer", "feat", None),
            P("layer", None, None, None),
            P("layer", None, None, None),
        ),
        out_specs=P("layer", "feat", None),
        check_vma=False,
    )
```

time: 215 us -> 221 us (1.028)
  Pallas kernels: 211 us -> 219 us
    pallas_call x1, Pallas kernels: 211 us -> 219 us  [local(): pl.pallas_call(functools.partial(kernel, nl, nb, nch, lent), out_shape=ja...]
where the time goes in v1:
time: 221 us
  Pallas kernels  219 us (99%)
  local copies, waits for them, and re-layouts  2.7 us (1%)
    pallas_call x1, Pallas kernels, local(): pl.pallas_call(functools.partial(kernel, nl, nb, nch, lent), out_shape=ja...  219 us

profile of v1, /device:TPU:7, one launch (start us, length us, event | category | flops | bytes accessed | tf_op | source)
XLA Modules:
  0.0 221.3 jit_solution(5949439870659045615)
XLA Ops:
  0.0 218.6 %shard_map.64 = bf16[320,2560]{1,0:T(8,128)(2,1)} custom-call(bf16[320,2560]{1,0:T(8,128)(2,1)} %bitcast.8, bf16[320,2560]{1,0:T(8,128)(2,1)} %bitcast.9, bf16[320,2560]{1,0:T(8,128)(2,1)} %bitcast.10, bf16[320,2560]{1,0:T(8,128)(2,1)} %bitcast.11, bf16[20,128,128]{2,1,0:T(8,128)(2,1)} %bitcast.12, bf16[20,128,128]{2,1,0:T(8,128)(2,1)} %bitcast.13), custom_call_target="tpu_custom_call" | custom-call | tf_op jit(solution)/shard_map/pallas_call | solution.py:483
  218.6 2.7 %copy.8 = bf16[1,320,2560]{2,1,0:T(8,128)(2,1)} copy(bf16[1,320,2560]{2,1,0:T(8,128)(2,1)} %bitcast.7) | data formatting | bytes 3276800

commit v2 on v1

--- a/solution.py
+++ b/solution.py
@@ -10,8 +10,23 @@
 MESH = pl.DeviceIdType.MESH
 BF = jnp.bfloat16
 F32 = jnp.float32
-LENT = 7
+LENT = 6
 HOLD = 3
+AHEAD = 2
+DELAY = 0
+SHIFT = 2
+HOME_RATE = 2
+AWAY_RATE = 3
+AWAY_WAIT = 4
+IDLE_ABOVE = 1
+IDLE_WAIT = 6
+IDLE_OWN = 4
+OWN_EARLY = 0
+IDLE_GAP = 2
+S_STEP = 4
+K_STEP = 6
+IDLE_S = 8
+IDLE_K = 9
 
 
 def kernel(nl, nb, nch, lent, g_ref, s_ref, c_ref, k_ref, oi_ref, ps_ref, out_ref,
@@ -36,11 +51,11 @@
     core_mate = (2 * a + 1 - c, f)
     swap_mate = (l, 2 * b + 1 - p)
     n_lag = nb - 1
-    r_lag = 2 * (nb - 1)
-    ahead = min(4, nch)
+    r_lag = 2 * (nb - 1) + DELAY + SHIFT - 1
+    ahead = min(AHEAD, nch)
     first_lent = nch - lent
-    halves = w2_send.shape[0]
-    piece = r // halves
+    parts = w2_send.shape[0]
+    piece = r // parts
 
     def remote(src, dst, ss, rs, dev):
         return pltpu.make_async_remote_copy(
@@ -63,18 +78,30 @@
     @pl.when(b < nb - 1)
     def _():
         pl.semaphore_signal(barrier, inc=1, device_id=(l, f + 2), device_id_type=MESH)
-
-    pl.semaphore_wait(barrier, 2 * nl - 1 + jnp.where(b > 0, 1, 0) + jnp.where(b < nb - 1, 1, 0))
 
     is_end = (b == 0) | (b == nb - 1)
     helps = (b == 1) | (b == nb - 2)
     if not lent:
         is_end = helps = b < 0
     mate_b = jnp.where(b < 2, 1 - b, 2 * nb - 3 - b)
-    mate = (l, 2 * mate_b + p)
+
+    @pl.when(is_end | helps)
+    def _():
+        for core, q in ((c, 1 - p), (1 - c, p), (1 - c, 1 - p)):
+            pl.semaphore_signal(barrier, inc=1, device_id=(2 * a + core, 2 * mate_b + q), device_id_type=MESH)
+
+    pl.semaphore_wait(barrier, 2 * nl - 1 + jnp.where(b > 0, 1, 0) + jnp.where(b < nb - 1, 1, 0)
+                      + jnp.where(is_end | helps, 3, 0))
 
     def is_lent(k):
         return chained & (k >= first_lent)
+
+    lends = is_end & (l < nl - 1)
+
+    def at(tt, shift):
+        late = chained & (tt >= first_lent)
+        k = jnp.where(late, tt - shift, tt)
+        return jnp.where((k >= nch) | (late & (k < first_lent)), -1, k)
 
     low = l + nl - 1
     low_a, low_p = (low - nl) // 2, lax.rem(low, 2)
@@ -104,15 +131,35 @@
         return remote(own_cols(hh, k), gl.at[k, p], gl_send.at[k, i], gl_recv.at[k, p], dev)
 
     def send_own(k, carry):
-        @pl.when(home)
+        keeps = jnp.logical_not(lends & (k >= first_lent))
+
+        @pl.when(home & keeps)
         def _():
             pltpu.make_async_copy(own_cols(c, k), gl.at[k, p], gl_recv.at[k, p]).start()
             own_to(1 - c, k, 0, core_mate).start()
 
-        @pl.when(away)
+        @pl.when(away & keeps)
         def _():
             own_to(c, k, 0, swap_mate).start()
             own_to(1 - c, k, 1, (2 * a + 1 - c, 2 * b + 1 - p)).start()
+        return carry
+
+    helper_q = jnp.where(home, p, 1 - p)
+
+    def lend_own(k, i):
+        core = c if i == 0 else 1 - c
+        return remote(own_cols(core, k), gl2.at[k - first_lent, p], gl2_send.at[k - first_lent, i],
+                      gl2_recv.at[k - first_lent, p], (2 * a + core, 2 * mate_b + helper_q))
+
+    def rows(i):
+        return pl.ds(pl.multiple_of(i * piece, piece), piece)
+
+    def lend_weight(i):
+        return remote(c_ref.at[rows(i)], w2.at[p, rows(i)], w2_send.at[i], w2_recv.at[p, i],
+                      (l, 2 * mate_b + helper_q))
+
+    def start_lend(i, carry):
+        lend_weight(i).start()
         return carry
 
     weights = (c_ref, s_ref, k_ref)
@@ -139,13 +186,10 @@
         remote(ps_ref.at[pl.ds((1 - c) * hb, hb)], tab.at[0], t_send.at[0], t_recv.at[0], core_mate).start()
         remote(oi_ref.at[pl.ds((1 - c) * hb, hb)], tab.at[1], t_send.at[1], t_recv.at[1], core_mate).start()
 
-    lax.fori_loop(0, ahead, send_own, 0)
+    send_own(0, 0)
     send_weight(0)
-    lax.fori_loop(ahead, nch, send_own, 0)
-    send_weight(1)
-    send_weight(2)
-
-    def take_weight(m, early):
+
+    def take_weight(m):
         @pl.when(used(m, role))
         def _():
             arrived(w.at[m, 1 - p], w_recv.at[m, 1 - p])
@@ -154,9 +198,7 @@
             def _():
                 remote(w.at[m, 1 - p], w.at[m, 1 - p], w_fwd.at[m], w_recv.at[m, 1 - p], core_mate).start()
 
-            @pl.when((not early) | away)
-            def _():
-                arrived(w.at[m, p], w_recv.at[m, p])
+            arrived(w.at[m, p], w_recv.at[m, p])
 
     def hop(buf, k, src, up, send, recv):
         dev = (l, f + 2) if up else (l, f - 2)
@@ -234,18 +276,19 @@
                  for i in range(per)]
         n_all[k, b] = jnp.concatenate(parts, axis=1) if per > 1 else parts[0]
 
-    def lend_own(k):
-        return remote(gl.at[k], gl2.at[k - first_lent], gl2_send.at[k - first_lent],
-                      gl2_recv.at[k - first_lent], mate)
-
-    def rows(i):
-        return pl.ds(i * piece, piece)
-
-    def lend_weight(i):
-        return remote(w.at[0, c, rows(i)], w2.at[c, rows(i)], w2_send.at[i], w2_recv.at[i], mate)
-
-    def share_weight(i):
-        return remote(w2.at[c, rows(i)], w2.at[c, rows(i)], w2_fwd.at[i], w2_got.at[i], core_mate)
+    def share_weight(q):
+        return remote(w2.at[q], w2.at[q], w2_fwd.at[q], w2_got.at[q], core_mate)
+
+    def take_lent():
+        for q in range(2):
+            @pl.when(home)
+            def _():
+                def got(i, carry):
+                    arrived(w2.at[q, rows(i)], w2_recv.at[q, i])
+                    return carry
+
+                lax.fori_loop(0, parts, got, 0)
+                share_weight(q).start()
 
     def take_own(k):
         for q in range(2):
@@ -264,7 +307,8 @@
 
     def reduced_lent(k):
         i = k - first_lent
-        arrived(gl2.at[i], gl2_recv.at[i])
+        for q in range(2):
+            arrived(gl2.at[i, q], gl2_recv.at[i, q])
         x = n_all[k].reshape(nb * 2 * r, cw)
         coupled = jnp.dot(w2[...].reshape(2 * r, d), x, preferred_element_type=F32)
         r_all[k, mate_b] = (gl2[i].reshape(2 * r, cw).astype(F32) - coupled).astype(BF)
@@ -336,40 +380,52 @@
         return jnp.clip(jnp.minimum(t - r_lag + 1, 2 * (t - held + 1)), 0, nch)
 
     def step(t, carry):
-        @pl.when(t + ahead < nch)
-        def _():
-            send_above(t + ahead, 0)
-
-        @pl.when(chained & inside(t))
-        def _():
-            near_step(t)
-        for j in range(nb):
-            pass_near(t - j, j)
-
-        @pl.when((t == 1) & home & used(0, role))
-        def _():
-            arrived(w.at[0, p], w_recv.at[0, p])
-        kr = t - n_lag
-
-        @pl.when(kr == 0)
-        def _():
-            take_weight(0, True)
+        more = jnp.where(chained, at(t + ahead, SHIFT), jnp.where(t - IDLE_ABOVE < nch, t - IDLE_ABOVE, -1))
+
+        @pl.when(more >= ahead)
+        def _():
+            send_above(more, 0)
+        kn = at(t, SHIFT)
+        ko = jnp.where(chained, t + OWN_EARLY, t - IDLE_GAP)
+
+        @pl.when((ko >= 1) & (ko < nch))
+        def _():
+            send_own(ko, 0)
+        for m, busy, idle in ((1, S_STEP, IDLE_S), (2, K_STEP, IDLE_K)):
+            @pl.when(t == jnp.where(chained, busy, idle))
+            def _():
+                send_weight(m)
+
+        @pl.when(chained & (kn >= 0))
+        def _():
+            near_step(kn)
+        pass_near(kn, 0)
         if lent:
-            for i in range(halves):
-                @pl.when(chained & is_end & (t == jnp.where(home, 1, n_lag) + i))
-                def _():
-                    lend_weight(i).start()
-
-            @pl.when(is_end & inside(t - 1) & is_lent(t - 1))
-            def _():
-                take_own(t - 1)
-                lend_own(t - 1).start()
-
-            @pl.when(chained & helps & (kr == first_lent))
-            def _():
-                for i in range(halves):
-                    arrived(w2.at[c, rows(i)], w2_recv.at[i])
-                    share_weight(i).start()
+            @pl.when(lends)
+            def _():
+                def upto(u):
+                    return jnp.clip(jnp.where(home, HOME_RATE * u, AWAY_RATE * (u - jnp.where(chained, AWAY_WAIT, IDLE_WAIT))), 0, parts)
+
+                lax.fori_loop(upto(t), upto(t + 1), start_lend, 0)
+
+            kg = jnp.where(chained, kn, t - IDLE_OWN)
+
+            @pl.when(lends & (kg >= first_lent) & (kg < nch))
+            def _():
+                for i in range(2):
+                    lend_own(kg, i).start()
+        for j in range(1, nb):
+            pass_near(at(t - j, SHIFT), j)
+
+        kr = at(t - n_lag - DELAY, SHIFT - 1)
+
+        @pl.when(t == n_lag + DELAY)
+        def _():
+            take_weight(0)
+        if lent:
+            @pl.when(chained & helps & (t == first_lent + n_lag + DELAY + SHIFT - 2))
+            def _():
+                take_lent()
 
         @pl.when(inside(kr) & jnp.logical_not(is_lent(kr) & is_end))
         def _():
@@ -377,21 +433,21 @@
             reduced_step(kr)
         pass_reduced(kr, 0)
         if lent:
-            @pl.when(chained & helps & (kr == first_lent))
-            def _():
-                for i in range(halves):
-                    arrived(w2.at[1 - c, rows(i)], w2_got.at[i])
+            @pl.when(chained & helps & away & (kr == first_lent))
+            def _():
+                for q in range(2):
+                    arrived(w2.at[q], w2_got.at[q])
 
             @pl.when(helps & inside(kr) & is_lent(kr))
             def _():
                 reduced_lent(kr)
         for j in range(1, nb):
-            pass_reduced(kr - j, j)
+            pass_reduced(at(t - n_lag - DELAY - j, SHIFT - 1), j)
 
         @pl.when(t == held)
         def _():
-            take_weight(1, False)
-            take_weight(2, False)
+            take_weight(1)
+            take_weight(2)
         lax.fori_loop(finals(t - 1), finals(t), final_step, 0)
         lax.fori_loop(finals(t - 2), finals(t - 1), out_step, 0)
         return carry
@@ -429,27 +485,36 @@
             @pl.when(chained & jnp.logical_not(stays(q, role + 1)))
             def _():
                 push_copy(k, q).wait_send()
-        own_to(c, k, 0, swap_mate).wait_send()
-
-        @pl.when(away)
+        gives = lends & (k >= first_lent)
+
+        @pl.when(jnp.logical_not(gives))
+        def _():
+            own_to(c, k, 0, swap_mate).wait_send()
+
+        @pl.when(away & jnp.logical_not(gives))
         def _():
             own_to(c, k, 1, swap_mate).wait_send()
         if lent:
-            @pl.when(is_lent(k) & is_end)
-            def _():
-                lend_own(k).wait_send()
+            @pl.when(gives)
+            def _():
+                for i in range(2):
+                    lend_own(k, i).wait_send()
         return carry
 
     lax.fori_loop(0, nch, drain, 0)
     if lent:
-        for i in range(halves):
-            @pl.when(chained & is_end)
-            def _():
-                lend_weight(i).wait_send()
-
-            @pl.when(chained & helps)
-            def _():
-                share_weight(i).wait_send()
+        def lent_out(i, carry):
+            lend_weight(i).wait_send()
+            return carry
+
+        @pl.when(lends)
+        def _():
+            lax.fori_loop(0, parts, lent_out, 0)
+
+        @pl.when(chained & helps & home)
+        def _():
+            for q in range(2):
+                share_weight(q).wait_send()
 
     @pl.when(home)
     def _():
@@ -476,7 +541,7 @@
     cw = h // nch
     lent = nch * LENT // 10 if nb >= 4 and nch >= 4 else 0
     keep = max(lent, 1)
-    halves = 2 if r % 32 == 0 else 1
+    parts = r // 32 if r % 32 == 0 else r // 16 if r % 16 == 0 else 1
     dma = pltpu.SemaphoreType.DMA
     vm = pltpu.VMEM
     anyspec = pl.BlockSpec(memory_space=pl.ANY)
@@ -494,7 +559,7 @@
             dma((2,)), dma((2,)),
             dma((nch, nb)), dma((nch, nb, 2)), dma((nch, nb)), dma((nch, nb, 2)),
             dma((nch, 2)), dma((nch, 2)), dma((nch, 2)), dma((nch, 2)),
-            dma((halves,)), dma((halves,)), dma((halves,)), dma((halves,)), dma((keep,)), dma((keep,)),
+            dma((2, parts)), dma((parts,)), dma((2,)), dma((2,)), dma((keep, 2)), dma((keep, 2)),
         ],
         compiler_params=pltpu.CompilerParams(
             collective_id=0, has_side_effects=True, vmem_limit_bytes=62 * 1024 * 1024),

time: 221 us -> 203 us (0.919)
  Pallas kernels: 219 us -> 200 us
    pallas_call x1, Pallas kernels: 219 us -> 200 us  [local(): pl.pallas_call(functools.partial(kernel, nl, nb, nch, lent), out_shape=ja...]
where the time goes in v2:
time: 203 us
  Pallas kernels  200 us (99%)
  local copies, waits for them, and re-layouts  2.7 us (1%)
    pallas_call x1, Pallas kernels, local(): pl.pallas_call(functools.partial(kernel, nl, nb, nch, lent), out_shape=ja...  200 us

profile of v2, /device:TPU:7, one launch (start us, length us, event | category | flops | bytes accessed | tf_op | source)
XLA Modules:
  0.0 202.8 jit_solution(15686366985378092326)
XLA Ops:
  0.0 200.1 %shard_map.64 = bf16[320,2560]{1,0:T(8,128)(2,1)} custom-call(bf16[320,2560]{1,0:T(8,128)(2,1)} %bitcast.8, bf16[320,2560]{1,0:T(8,128)(2,1)} %bitcast.9, bf16[320,2560]{1,0:T(8,128)(2,1)} %bitcast.10, bf16[320,2560]{1,0:T(8,128)(2,1)} %bitcast.11, bf16[20,128,128]{2,1,0:T(8,128)(2,1)} %bitcast.12, bf16[20,128,128]{2,1,0:T(8,128)(2,1)} %bitcast.13), custom_call_target="tpu_custom_call" | custom-call | tf_op jit(solution)/shard_map/pallas_call | solution.py:548
  200.1 2.7 %copy.8 = bf16[1,320,2560]{2,1,0:T(8,128)(2,1)} copy(bf16[1,320,2560]{2,1,0:T(8,128)(2,1)} %bitcast.7) | data formatting | bytes 3276800

commit v3 on v2

--- a/solution.py
+++ b/solution.py
@@ -54,7 +54,7 @@
     r_lag = 2 * (nb - 1) + DELAY + SHIFT - 1
     ahead = min(AHEAD, nch)
     first_lent = nch - lent
-    parts = w2_send.shape[0]
+    parts = r // 32 if r % 32 == 0 else r // 16 if r % 16 == 0 else 1
     piece = r // parts
 
     def remote(src, dst, ss, rs, dev):
@@ -113,14 +113,14 @@
         return (l >= 1) & (c == 1) & (p == 0) & (c == hh)
 
     def above_copy(hh, k):
-        return remote(own_cols(hh, k), gn.at[k, p], gn_send.at[k, hh], gn_recv.at[k, p],
+        return remote(own_cols(hh, k), gn.at[k, p], gn_send.at[hh], gn_recv.at[k],
                       (2 * low_a + hh, 2 * b + low_p))
 
     def send_above(k, carry):
         for hh in range(2):
             @pl.when(above_stays(hh))
             def _():
-                pltpu.make_async_copy(own_cols(hh, k), gn.at[k, p], gn_recv.at[k, p]).start()
+                pltpu.make_async_copy(own_cols(hh, k), gn.at[k, p], gn_recv.at[k]).start()
 
             @pl.when((l >= 1) & jnp.logical_not(above_stays(hh)))
             def _():
@@ -128,14 +128,14 @@
         return carry
 
     def own_to(hh, k, i, dev):
-        return remote(own_cols(hh, k), gl.at[k, p], gl_send.at[k, i], gl_recv.at[k, p], dev)
+        return remote(own_cols(hh, k), gl.at[k, p], gl_send.at[i], gl_recv.at[k], dev)
 
     def send_own(k, carry):
         keeps = jnp.logical_not(lends & (k >= first_lent))
 
         @pl.when(home & keeps)
         def _():
-            pltpu.make_async_copy(own_cols(c, k), gl.at[k, p], gl_recv.at[k, p]).start()
+            pltpu.make_async_copy(own_cols(c, k), gl.at[k, p], gl_recv.at[k]).start()
             own_to(1 - c, k, 0, core_mate).start()
 
         @pl.when(away & keeps)
@@ -148,14 +148,14 @@
 
     def lend_own(k, i):
         core = c if i == 0 else 1 - c
-        return remote(own_cols(core, k), gl2.at[k - first_lent, p], gl2_send.at[k - first_lent, i],
-                      gl2_recv.at[k - first_lent, p], (2 * a + core, 2 * mate_b + helper_q))
+        return remote(own_cols(core, k), gl2.at[k - first_lent, p], gl2_send.at[i],
+                      gl2_recv.at[k - first_lent], (2 * a + core, 2 * mate_b + helper_q))
 
     def rows(i):
         return pl.ds(pl.multiple_of(i * piece, piece), piece)
 
     def lend_weight(i):
-        return remote(c_ref.at[rows(i)], w2.at[p, rows(i)], w2_send.at[i], w2_recv.at[p, i],
+        return remote(c_ref.at[rows(i)], w2.at[p, rows(i)], w2_send.at[0], w2_recv.at[p],
                       (l, 2 * mate_b + helper_q))
 
     def start_lend(i, carry):
@@ -202,7 +202,7 @@
 
     def hop(buf, k, src, up, send, recv):
         dev = (l, f + 2) if up else (l, f - 2)
-        return remote(buf.at[k, src], buf.at[k, src], send.at[k, src, 0 if up else 1], recv.at[k, src], dev)
+        return remote(buf.at[k, src], buf.at[k, src], send.at[src, 0 if up else 1], recv.at[k, src], dev)
 
     def n_up(k):
         return (b < nb - 1) & jnp.logical_not(is_lent(k) & (b + 1 == nb - 1))
@@ -268,8 +268,7 @@
         arrived(tab.at[i], t_recv.at[i])
 
     def near_step(k):
-        for q in range(2):
-            arrived(gn.at[k, q], gn_recv.at[k, q])
+        arrived(gn.at[k], gn_recv.at[k])
         x = gn[k].reshape(2 * r, cw)
         parts = [lax.dot_general(x[:, i * blk:(i + 1) * blk], tab[0, k * per + i],
                                  (((1,), (1,)), ((), ())), preferred_element_type=F32).astype(BF)
@@ -283,16 +282,11 @@
         for q in range(2):
             @pl.when(home)
             def _():
-                def got(i, carry):
-                    arrived(w2.at[q, rows(i)], w2_recv.at[q, i])
-                    return carry
-
-                lax.fori_loop(0, parts, got, 0)
+                arrived(w2.at[q], w2_recv.at[q])
                 share_weight(q).start()
 
     def take_own(k):
-        for q in range(2):
-            arrived(gl.at[k, q], gl_recv.at[k, q])
+        arrived(gl.at[k], gl_recv.at[k])
 
     def reduced_step(k):
         @pl.when(chained)
@@ -307,8 +301,7 @@
 
     def reduced_lent(k):
         i = k - first_lent
-        for q in range(2):
-            arrived(gl2.at[i, q], gl2_recv.at[i, q])
+        arrived(gl2.at[i], gl2_recv.at[i])
         x = n_all[k].reshape(nb * 2 * r, cw)
         coupled = jnp.dot(w2[...].reshape(2 * r, d), x, preferred_element_type=F32)
         r_all[k, mate_b] = (gl2[i].reshape(2 * r, cw).astype(F32) - coupled).astype(BF)
@@ -316,10 +309,10 @@
             hop(r_all, k, mate_b, up, r_send, r_recv).start()
 
     def local_copy(k, q):
-        return remote(l_st.at[k, q], l_in.at[k, c], l_send.at[k, q], l_recv.at[k, c], (role, 2 * b + q))
+        return remote(l_st.at[k, q], l_in.at[k, c], l_send.at[q], l_recv.at[k], (role, 2 * b + q))
 
     def push_copy(k, q):
-        return remote(p_st.at[k, q], p_in.at[k, c], p_send.at[k, q], p_recv.at[k, c],
+        return remote(p_st.at[k, q], p_in.at[k, c], p_send.at[q], p_recv.at[k],
                       (lax.rem(role + 1, nl), 2 * b + q))
 
     def stays(q, layer):
@@ -334,7 +327,7 @@
         for q in range(2):
             @pl.when(stays(q, role))
             def _():
-                pltpu.make_async_copy(l_st.at[k, q], l_in.at[k, c], l_recv.at[k, c]).start()
+                pltpu.make_async_copy(l_st.at[k, q], l_in.at[k, c], l_recv.at[k]).start()
 
             @pl.when(jnp.logical_not(stays(q, role)))
             def _():
@@ -352,7 +345,7 @@
             for q in range(2):
                 @pl.when(stays(q, role + 1))
                 def _():
-                    pltpu.make_async_copy(p_st.at[k, q], p_in.at[k, c], p_recv.at[k, c]).start()
+                    pltpu.make_async_copy(p_st.at[k, q], p_in.at[k, c], p_recv.at[k]).start()
 
                 @pl.when(jnp.logical_not(stays(q, role + 1)))
                 def _():
@@ -360,13 +353,16 @@
         return carry
 
     def out_step(k, carry):
+        arrived(l_in.at[k], l_recv.at[k])
+
+        @pl.when(l > 0)
+        def _():
+            arrived(p_in.at[k], p_recv.at[k])
         for hh in range(2):
-            arrived(l_in.at[k, hh], l_recv.at[k, hh])
             dst = pl.ds(pl.multiple_of(hh * h + k * cw, cw), cw)
 
             @pl.when(l > 0)
             def _():
-                arrived(p_in.at[k, hh], p_recv.at[k, hh])
                 out_ref[:, dst] = (l_in[k, hh].astype(F32) - p_in[k, hh].astype(F32)).astype(BF)
 
             @pl.when(l == 0)
@@ -454,62 +450,35 @@
 
     lax.fori_loop(0, nch + r_lag + 1, step, 0)
 
-    def drain(k, carry):
-        for src in range(nb):
-            @pl.when(chained & (src <= b) & n_up(k) & jnp.logical_not(is_lent(k) & is_end & (src != b)))
-            def _():
-                hop(n_all, k, src, True, n_send, n_recv).wait_send()
-
-            @pl.when(chained & (src >= b) & n_down(k) & jnp.logical_not(is_lent(k) & is_end & (src != b)))
-            def _():
-                hop(n_all, k, src, False, n_send, n_recv).wait_send()
-            kept = is_lent(k) & is_end & (src == b)
-            made = is_lent(k) & helps & (src == mate_b)
-
-            @pl.when((b < nb - 1) & (src <= b) & jnp.logical_not(kept) | made)
-            def _():
-                hop(r_all, k, src, True, r_send, r_recv).wait_send()
-
-            @pl.when((b > 0) & (src >= b) & jnp.logical_not(kept) | made)
-            def _():
-                hop(r_all, k, src, False, r_send, r_recv).wait_send()
-        for q in range(2):
-            @pl.when((l >= 1) & jnp.logical_not(above_stays(q)))
-            def _():
-                above_copy(q, k).wait_send()
-
-            @pl.when(jnp.logical_not(stays(q, role)))
-            def _():
-                local_copy(k, q).wait_send()
-
-            @pl.when(chained & jnp.logical_not(stays(q, role + 1)))
-            def _():
-                push_copy(k, q).wait_send()
-        gives = lends & (k >= first_lent)
-
-        @pl.when(jnp.logical_not(gives))
-        def _():
-            own_to(c, k, 0, swap_mate).wait_send()
-
-        @pl.when(away & jnp.logical_not(gives))
-        def _():
-            own_to(c, k, 1, swap_mate).wait_send()
-        if lent:
-            @pl.when(gives)
-            def _():
-                for i in range(2):
-                    lend_own(k, i).wait_send()
-        return carry
-
-    lax.fori_loop(0, nch, drain, 0)
+    def settle(ok, buf, count, sem):
+        if count:
+            @pl.when(ok)
+            def _():
+                arrived(buf.at[pl.ds(0, count)], sem)
+
+    for src in range(nb):
+        for i, (on, edge) in enumerate((((src <= b) & (b < nb - 1), b + 1 == nb - 1),
+                                        ((src >= b) & (b > 0), b - 1 == 0))):
+            short = edge if lent else b < 0
+            settle(chained & on & jnp.logical_not(short), n_all.at[:, src], nch, n_send.at[src, i])
+            settle(chained & on & short, n_all.at[:, src], first_lent, n_send.at[src, i])
+            kept = chained & is_end & (src == b)
+            settle(on & jnp.logical_not(kept), r_all.at[:, src], nch, r_send.at[src, i])
+            settle(on & kept, r_all.at[:, src], first_lent, r_send.at[src, i])
+            made = chained & helps & (src == mate_b) & jnp.logical_not(on)
+            settle(made, r_all.at[:, src], lent, r_send.at[src, i])
+    for q in range(2):
+        settle((l >= 1) & jnp.logical_not(above_stays(q)), gn.at[:, 0], nch, gn_send.at[q])
+        settle(jnp.logical_not(stays(q, role)), l_st.at[:, q], nch, l_send.at[q])
+        settle(chained & jnp.logical_not(stays(q, role + 1)), p_st.at[:, q], nch, p_send.at[q])
+        sends = away if q else home | away
+        settle(sends & jnp.logical_not(lends), gl.at[:, 0], nch, gl_send.at[q])
+        settle(sends & lends, gl.at[:, 0], first_lent, gl_send.at[q])
+        settle(lends, gl2.at[:, 0], lent, gl2_send.at[q])
     if lent:
-        def lent_out(i, carry):
-            lend_weight(i).wait_send()
-            return carry
-
         @pl.when(lends)
         def _():
-            lax.fori_loop(0, parts, lent_out, 0)
+            arrived(w2.at[0], w2_send.at[0])
 
         @pl.when(chained & helps & home)
         def _():
@@ -541,13 +510,12 @@
     cw = h // nch
     lent = nch * LENT // 10 if nb >= 4 and nch >= 4 else 0
     keep = max(lent, 1)
-    parts = r // 32 if r % 32 == 0 else r // 16 if r % 16 == 0 else 1
     dma = pltpu.SemaphoreType.DMA
     vm = pltpu.VMEM
     anyspec = pl.BlockSpec(memory_space=pl.ANY)
     out = pl.pallas_call(
         functools.partial(kernel, nl, nb, nch, lent),
-        out_shape=jax.ShapeDtypeStruct((r, d), BF),
+        out_shape=pltpu.VMEM((r, d), BF),
         in_specs=[anyspec] * 6,
         out_specs=pl.BlockSpec(memory_space=pltpu.VMEM),
         scratch_shapes=[
@@ -555,11 +523,11 @@
             vm((nch, nb, 2 * r, cw), BF), vm((nch, nb, 2 * r, cw), BF),
             vm((nch, 2, r, cw), BF), vm((nch, 2, r, cw), BF), vm((nch, 2, r, cw), BF), vm((nch, 2, r, cw), BF),
             vm((2, r, d), BF), vm((keep, 2, r, cw), BF),
-            dma((3, 2)), dma((3,)), dma((3,)), dma((nch, 2)), dma((nch, 2)), dma((nch, 2)), dma((nch, 2)),
+            dma((3, 2)), dma((3,)), dma((3,)), dma((nch,)), dma((2,)), dma((nch,)), dma((2,)),
             dma((2,)), dma((2,)),
-            dma((nch, nb)), dma((nch, nb, 2)), dma((nch, nb)), dma((nch, nb, 2)),
-            dma((nch, 2)), dma((nch, 2)), dma((nch, 2)), dma((nch, 2)),
-            dma((2, parts)), dma((parts,)), dma((2,)), dma((2,)), dma((keep, 2)), dma((keep, 2)),
+            dma((nch, nb)), dma((nb, 2)), dma((nch, nb)), dma((nb, 2)),
+            dma((nch,)), dma((2,)), dma((nch,)), dma((2,)),
+            dma((2,)), dma((1,)), dma((2,)), dma((2,)), dma((keep,)), dma((2,)),
         ],
         compiler_params=pltpu.CompilerParams(
             collective_id=0, has_side_effects=True, vmem_limit_bytes=62 * 1024 * 1024),

time: 203 us -> 196 us (0.966)
  Pallas kernels: 200 us -> 195 us
    pallas_call x1, Pallas kernels: 200 us -> 195 us  [local(): pl.pallas_call(functools.partial(kernel, nl, nb, nch, lent), out_shape=pl...]
where the time goes in v3:
time: 196 us
  Pallas kernels  195 us (99%)
    pallas_call x1, Pallas kernels, local(): pl.pallas_call(functools.partial(kernel, nl, nb, nch, lent), out_shape=pl...  195 us

profile of v3, /device:TPU:7, one launch (start us, length us, event | category | flops | bytes accessed | tf_op | source)
XLA Modules:
  0.0 196.3 jit_solution(2419892773988446491)
XLA Ops:
  0.0 195.1 %shard_map.64 = bf16[320,2560]{1,0:T(8,128)(2,1)S(1)} custom-call(bf16[320,2560]{1,0:T(8,128)(2,1)} %bitcast.8, bf16[320,2560]{1,0:T(8,128)(2,1)} %bitcast.9, bf16[320,2560]{1,0:T(8,128)(2,1)} %bitcast.10, bf16[320,2560]{1,0:T(8,128)(2,1)} %bitcast.11, bf16[20,128,128]{2,1,0:T(8,128)(2,1)} %bitcast.12, bf16[20,128,128]{2,1,0:T(8,128)(2,1)} %bitcast.13), custom_call_target="tpu_custom_call" | custom-call | tf_op jit(solution)/shard_map/pallas_call | solution.py:516
  195.1 1.2 copy.8

commit v4 on v3

--- a/solution.py
+++ b/solution.py
@@ -16,10 +16,10 @@
 DELAY = 0
 SHIFT = 2
 HOME_RATE = 2
-AWAY_RATE = 3
+AWAY_RATE = 4
 AWAY_WAIT = 4
-IDLE_ABOVE = 1
-IDLE_WAIT = 6
+IDLE_ABOVE = 2
+IDLE_WAIT = 7
 IDLE_OWN = 4
 OWN_EARLY = 0
 IDLE_GAP = 2

time: 196 us -> 188 us (0.959)
  Pallas kernels: 195 us -> 187 us
    pallas_call x1, Pallas kernels: 195 us -> 187 us  [local(): pl.pallas_call(functools.partial(kernel, nl, nb, nch, lent), out_shape=pl...]
where the time goes in v4:
time: 188 us
  Pallas kernels  187 us (99%)
    pallas_call x1, Pallas kernels, local(): pl.pallas_call(functools.partial(kernel, nl, nb, nch, lent), out_shape=pl...  187 us

profile of v4, /device:TPU:7, one launch (start us, length us, event | category | flops | bytes accessed | tf_op | source)
XLA Modules:
  0.0 188.0 jit_solution(9967345867140601921)
XLA Ops:
  0.0 186.8 %shard_map.64 = bf16[320,2560]{1,0:T(8,128)(2,1)S(1)} custom-call(bf16[320,2560]{1,0:T(8,128)(2,1)} %bitcast.8, bf16[320,2560]{1,0:T(8,128)(2,1)} %bitcast.9, bf16[320,2560]{1,0:T(8,128)(2,1)} %bitcast.10, bf16[320,2560]{1,0:T(8,128)(2,1)} %bitcast.11, bf16[20,128,128]{2,1,0:T(8,128)(2,1)} %bitcast.12, bf16[20,128,128]{2,1,0:T(8,128)(2,1)} %bitcast.13), custom_call_target="tpu_custom_call" | custom-call | tf_op jit(solution)/shard_map/pallas_call | solution.py:516
  186.8 1.2 copy.8
